TPU v7x, 32 devices: a whole 2x2x4 slice. The times are simulated.
32 devices in a mesh: req: 2 (over y), tm: 4 (over z), rows: 2 (over x), sub: 2 (over core).
Axes of the slice: x: 2, y: 2, z: 4, core: 2. Of those that a mesh axis runs over, the one named last changes fastest.
Arguments:
- latents: bfloat16 [32, 256, 640], P('tm', ('req', 'rows')), parts along dimension 1, may hold values from -6 to 6
- cotangent: bfloat16 [32, 256, 640], P('tm', ('req', 'rows')), parts along dimension 1, may hold values from -6 to 6
- w_qkv: bfloat16 [640, 3, 640], P(None, None, 'sub'), may hold values from -0.25 to 0.25
- w_out: bfloat16 [640, 640], P('sub'), may hold values from -0.25 to 0.25
- time_bias: float32 [8, 63], replicated, may hold values from -4 to 310
Outputs:
- grad_latents: bfloat16 [32, 256, 640], P('tm', ('req', 'rows'), 'sub'), parts along dimension 1
- grad_w_qkv: float32 [1280, 3, 640], P(('req', 'tm', 'rows'), None, 'sub'), parts along dimension 0
- grad_w_out_t: float32 [1280, 640], P(('req', 'tm', 'rows'), 'sub'), parts along dimension 0
There are 2 independent parts, one for each index of `req`. A program takes and returns all parts, laid end to end along the dimension named above; an argument that names none is the same for every part. Nothing has to cross between parts.
All inputs are finite; a program needn't handle non-finite values.
Results may differ from a plain program's by a relative error of at most 0.012.
Values may be sent and summed in bfloat16 or wider, within the bound.
No kernel may reach another device: no remote copies, remote signals or barrier semaphores. Data moves between devices by JAX's collectives and lax.ppermute only.
A program may use at most 128 MiB of HBM per device.

v0:
```python
import math
import jax
import jax.numpy as jnp
from jax import lax
from jax.sharding import PartitionSpec as P

H = 8


def positional(frame_pos, channels):
    half = channels // 2
    frequency = jnp.exp(-math.log(10000.0) * jnp.arange(half, dtype=jnp.float32) * 2.0 / channels)
    angles = frame_pos.astype(jnp.float32)[:, None] * frequency[None, :]
    return jnp.concatenate((jnp.sin(angles), jnp.cos(angles)), axis=1)


def bias_table(bias_rows, frames):
    offsets = (
        jnp.arange(frames, dtype=jnp.int32)[:, None]
        - jnp.arange(frames, dtype=jnp.int32)[None, :]
        + frames
        - 1
    )
    return bias_rows[:, offsets]


def embed(latents, frame_pos):
    return (
        latents.astype(jnp.float32) + positional(frame_pos, latents.shape[2])[:, None, :]
    ).astype(jnp.bfloat16)


def project(hidden, w_qkv, cotangent, w_out):
    qkv = jnp.einsum("fsc,ctd->fstd", hidden, w_qkv, preferred_element_type=jnp.float32).astype(
        jnp.bfloat16
    )
    grad_attn = jnp.einsum(
        "fse,de->fsd", cotangent, w_out, preferred_element_type=jnp.float32
    ).astype(jnp.bfloat16)
    return (qkv[:, :, 0], qkv[:, :, 1], qkv[:, :, 2], grad_attn)


def attend(query_rows, key_rows, value_rows, grad_rows, bias_rows, head_count):
    frames, positions, local_width = query_rows.shape
    head_size = local_width // head_count
    inv_root = 1.0 / math.sqrt(head_size)
    shape4 = (frames, positions, head_count, head_size)
    query_heads = query_rows.reshape(shape4)
    key_heads = key_rows.reshape(shape4)
    value_heads = value_rows.reshape(shape4)
    grad_heads = grad_rows.reshape(shape4)
    scores = (
        jnp.einsum("iphd,jphd->phij", query_heads, key_heads, preferred_element_type=jnp.float32)
        * inv_root
        + bias_rows[None]
    )
    row_max = jnp.max(scores, axis=-1, keepdims=True)
    raw_weights = jnp.exp(scores - row_max)
    probs = raw_weights / jnp.sum(raw_weights, axis=-1, keepdims=True)
    probs_low = probs.astype(jnp.bfloat16)
    attn_out = jnp.einsum(
        "phij,jphd->iphd", probs_low, value_heads, preferred_element_type=jnp.float32
    ).astype(jnp.bfloat16)
    grad_probs = jnp.einsum(
        "iphd,jphd->phij", grad_heads, value_heads, preferred_element_type=jnp.float32
    )
    row_dot = jnp.sum(probs * grad_probs, axis=-1, keepdims=True)
    grad_scores = (probs * (grad_probs - row_dot) * inv_root).astype(jnp.bfloat16)
    grad_query = jnp.einsum(
        "phij,jphd->iphd", grad_scores, key_heads, preferred_element_type=jnp.float32
    ).astype(jnp.bfloat16)
    grad_key = jnp.einsum(
        "phij,iphd->jphd", grad_scores, query_heads, preferred_element_type=jnp.float32
    ).astype(jnp.bfloat16)
    grad_value = jnp.einsum(
        "phij,iphd->jphd", probs_low, grad_heads, preferred_element_type=jnp.float32
    ).astype(jnp.bfloat16)
    flat = (frames, positions, local_width)
    return (
        attn_out.reshape(flat),
        grad_query.reshape(flat),
        grad_key.reshape(flat),
        grad_value.reshape(flat),
    )


def latent_grad(grad_qkv, w_qkv, cotangent, head_group):
    local_width = w_qkv.shape[2]
    back_term = jnp.einsum("fstd,ctd->fsc", grad_qkv, w_qkv, preferred_element_type=jnp.float32)
    summed_back = lax.psum_scatter(
        back_term.astype(jnp.bfloat16), "sub", scatter_dimension=2, tiled=True
    ).astype(jnp.float32)
    own_cotangent = lax.dynamic_slice_in_dim(cotangent, head_group * local_width, local_width, 2)
    return (own_cotangent.astype(jnp.float32) + summed_back).astype(jnp.bfloat16)


def per_device(latents, cotangent, w_qkv, w_out, time_bias):
    channels = latents.shape[2]
    local_width = w_qkv.shape[2]
    head_count = H // lax.axis_size("sub")
    head_group = lax.axis_index("sub")
    all_frames = latents.shape[0] * lax.axis_size("tm")
    bias_rows = bias_table(
        lax.dynamic_slice_in_dim(time_bias, head_group * head_count, head_count, 0), all_frames
    )
    frame_pos = lax.axis_index("tm") * latents.shape[0] + jnp.arange(
        latents.shape[0], dtype=jnp.int32
    )
    hidden = embed(latents, frame_pos)
    query_rows, key_rows, value_rows, grad_attn = project(hidden, w_qkv, cotangent, w_out)
    query_rows, key_rows, value_rows, grad_attn = (
        lax.all_to_all(query_rows, "tm", split_axis=1, concat_axis=0, tiled=True),
        lax.all_to_all(key_rows, "tm", split_axis=1, concat_axis=0, tiled=True),
        lax.all_to_all(value_rows, "tm", split_axis=1, concat_axis=0, tiled=True),
        lax.all_to_all(grad_attn, "tm", split_axis=1, concat_axis=0, tiled=True),
    )
    attn_out, grad_query, grad_key, grad_value = attend(
        query_rows, key_rows, value_rows, grad_attn, bias_rows, head_count
    )
    attn_out, grad_query, grad_key, grad_value = (
        lax.all_to_all(attn_out, "tm", split_axis=0, concat_axis=1, tiled=True),
        lax.all_to_all(grad_query, "tm", split_axis=0, concat_axis=1, tiled=True),
        lax.all_to_all(grad_key, "tm", split_axis=0, concat_axis=1, tiled=True),
        lax.all_to_all(grad_value, "tm", split_axis=0, concat_axis=1, tiled=True),
    )
    grad_qkv = jnp.stack((grad_query, grad_key, grad_value), axis=2)
    grad_latents = latent_grad(grad_qkv, w_qkv, cotangent, head_group)
    flat_hidden = hidden.reshape(-1, channels)
    flat_cotangent = cotangent.reshape(-1, channels)
    flat_grads = grad_qkv.reshape(-1, 3 * local_width)
    flat_out = attn_out.reshape(-1, local_width)
    qkv_part = lax.dot_general(
        flat_hidden, flat_grads, (((0,), (0,)), ((), ())), preferred_element_type=jnp.float32
    )
    out_part = lax.dot_general(
        flat_cotangent, flat_out, (((0,), (0,)), ((), ())), preferred_element_type=jnp.float32
    )
    summed_grads = lax.psum_scatter(
        jnp.concatenate((qkv_part, out_part), axis=1),
        ("tm", "rows"),
        scatter_dimension=0,
        tiled=True,
    )
    grad_w_qkv = summed_grads[:, : 3 * local_width].reshape(-1, 3, local_width)
    grad_w_out_t = summed_grads[:, 3 * local_width :]
    return (grad_latents, grad_w_qkv, grad_w_out_t)


def solution(mesh):
    return jax.shard_map(
        per_device,
        mesh=mesh,
        in_specs=(
            P("tm", ("req", "rows"), None),
            P("tm", ("req", "rows"), None),
            P(None, None, "sub"),
            P("sub", None),
            P(),
        ),
        out_specs=(
            P("tm", ("req", "rows"), "sub"),
            P(("req", "tm", "rows"), None, "sub"),
            P(("req", "tm", "rows"), "sub"),
        ),
        check_vma=False,
    )
```

profile of v0, /device:TPU:0, one launch (start us, length us, event | category | flops | bytes accessed | tf_op | source)
XLA Modules:
  0.0 233.2 jit_solution(9928908016868254245)
XLA Ops:
  10.0 6.3 %all-to-all-start.2 = ((bf16[8,64,320]{2,0,1:T(8,128)(2,1)}), bf16[8,64,320]{2,0,1:T(8,128)(2,1)S(1)}, u32[]{:S(2)}, u32[]{:S(2)}) async-start(bf16[8,64,320]{2,0,1:T(8,128)(2,1)} %copy.49), calls=%async_computation.2 | async-start | bytes 786432 | tf_op jit(solution)/shard_map/all_to_all | solution.py:115
  19.0 9.0 %all-to-all-done.2 = bf16[8,64,320]{2,0,1:T(8,128)(2,1)S(1)} async-done(((bf16[8,64,320]{2,0,1:T(8,128)(2,1)}), bf16[8,64,320]{2,0,1:T(8,128)(2,1)S(1)}, u32[]{:S(2)}, u32[]{:S(2)}) %all-to-all-start.2) | async-done | bytes 327712 | tf_op jit(solution)/shard_map/all_to_all | solution.py:115
  28.1 3.5 %all-to-all-start.3 = ((bf16[8,64,320]{2,0,1:T(8,128)(2,1)}), bf16[8,64,320]{2,0,1:T(8,128)(2,1)S(1)}, u32[]{:S(2)}, u32[]{:S(2)}) async-start(bf16[8,64,320]{2,0,1:T(8,128)(2,1)} %copy.51), calls=%async_computation.3 | async-start | bytes 786432 | tf_op jit(solution)/shard_map/all_to_all | solution.py:114
  32.5 9.9 %all-to-all-done.3 = bf16[8,64,320]{2,0,1:T(8,128)(2,1)S(1)} async-done(((bf16[8,64,320]{2,0,1:T(8,128)(2,1)}), bf16[8,64,320]{2,0,1:T(8,128)(2,1)S(1)}, u32[]{:S(2)}, u32[]{:S(2)}) %all-to-all-start.3) | async-done | bytes 327712 | tf_op jit(solution)/shard_map/all_to_all | solution.py:114
  42.4 3.5 %all-to-all-start.1 = ((bf16[8,64,320]{2,0,1:T(8,128)(2,1)}), bf16[8,64,320]{2,0,1:T(8,128)(2,1)S(1)}, u32[]{:S(2)}, u32[]{:S(2)}) async-start(bf16[8,64,320]{2,0,1:T(8,128)(2,1)} %copy.43), calls=%async_computation.1 | async-start | bytes 786432 | tf_op jit(solution)/shard_map/all_to_all | solution.py:112
  46.8 8.8 %all-to-all-done.1 = bf16[8,64,320]{2,0,1:T(8,128)(2,1)S(1)} async-done(((bf16[8,64,320]{2,0,1:T(8,128)(2,1)}), bf16[8,64,320]{2,0,1:T(8,128)(2,1)S(1)}, u32[]{:S(2)}, u32[]{:S(2)}) %all-to-all-start.1) | async-done | bytes 327712 | tf_op jit(solution)/shard_map/all_to_all | solution.py:112
  55.7 3.5 %all-to-all-start = ((bf16[8,64,320]{2,0,1:T(8,128)(2,1)}), bf16[8,64,320]{2,0,1:T(8,128)(2,1)S(1)}, u32[]{:S(2)}, u32[]{:S(2)}) async-start(bf16[8,64,320]{2,0,1:T(8,128)(2,1)} %copy.41), calls=%async_computation | async-start | bytes 786432 | tf_op jit(solution)/shard_map/all_to_all | solution.py:113
  59.4 4.0 %gather_fusion = f32[1024,4]{1,0:T(8,128)} fusion(f32[4,63]{0,1:T(8,128)S(1)} %copy.80, s32[1024]{0:T(1024)S(1)} %broadcast_clamp_fusion), kind=kCustom, calls=%fused_computation | custom fusion | bytes 36864 | tf_op jit(solution)/shard_map/gather | solution.py:24
  65.5 2.1 reshape.98
  73.8 2.5 %fusion.13 = bf16[32,16,4,80]{3,0,2,1:T(8,128)(2,1)} fusion(bf16[32,16,4,80]{3,2,1,0:T(4,128)(2,1)} %reshape.98, f32[16,4,32]{2,1,0:T(4,128)S(1)} %get-tuple-element.17, f32[16,4,32,32]{2,3,1,0:T(8,128)S(1)} %fusion.7), kind=kOutput, calls=%fused_computation.25 | convolution fusion | flops 10848287 | bytes 925696 | tf_op jit(solution)/shard_map/phij,iphd->jphd/dot_general | solution.py:75
  78.7 5.0 %all-to-all-start.6 = ((bf16[32,16,320]{2,1,0:T(8,128)(2,1)}), bf16[32,16,320]{2,1,0:T(8,128)(2,1)}, u32[]{:S(2)}, u32[]{:S(2)}) async-start(bf16[32,16,320]{2,1,0:T(8,128)(2,1)} %reshape.102), calls=%async_computation.6 | async-start | bytes 786432 | tf_op jit(solution)/shard_map/all_to_all | solution.py:124
  83.7 3.0 %fusion.27 = f32[16,4,32,32]{2,3,1,0:T(8,128)} fusion(bf16[32,16,4,80]{3,2,1,0:T(4,128)(2,1)} %reshape.99, bf16[32,16,4,80]{3,2,1,0:T(4,128)(2,1)} %reshape.98), kind=kOutput, calls=%fused_computation.39 | convolution fusion | flops 10485760 | bytes 917504 | tf_op jit(solution)/shard_map/iphd,jphd->phij/dot_general | solution.py:64
  86.7 3.7 %fusion.12 = bf16[32,16,4,80]{3,0,2,1:T(8,128)(2,1)} fusion(f32[16,4,32,32]{2,3,1,0:T(8,128)} %fusion.27, bf16[32,16,4,80]{3,2,1,0:T(4,128)(2,1)S(1)} %copy-done.3, f32[16,4,32,32]{2,3,1,0:T(8,128)} %get-tuple-element.18, f32[16,4,32]{2,1,0:T(4,128)S(1)} %get-tuple-element.17), kind=kOutput, calls=%fused_computation.24 | convolution fusion | flops 11110431 | bytes 1187840 | tf_op jit(solution)/shard_map/phij,iphd->jphd/dot_general | solution.py:72
  93.0 5.0 %all-to-all-start.5 = ((bf16[32,16,320]{2,1,0:T(8,128)(2,1)}), bf16[32,16,320]{2,1,0:T(8,128)(2,1)}, u32[]{:S(2)}, u32[]{:S(2)}) async-start(bf16[32,16,320]{2,1,0:T(8,128)(2,1)} %reshape.101), calls=%async_computation.5 | async-start | bytes 786432 | tf_op jit(solution)/shard_map/all_to_all | solution.py:123
  98.0 3.9 %fusion.10 = bf16[32,16,4,80]{3,0,2,1:T(8,128)(2,1)} fusion(f32[16,4,32,32]{2,3,1,0:T(8,128)} %fusion.27, bf16[32,16,4,80]{3,2,1,0:T(4,128)(2,1)} %copy-done.2, f32[16,4,32,32]{2,3,1,0:T(8,128)} %get-tuple-element.18, f32[16,4,32]{2,1,0:T(4,128)S(1)} %get-tuple-element.17), kind=kOutput, calls=%fused_computation.22 | convolution fusion | flops 11110431 | bytes 1187840 | tf_op jit(solution)/shard_map/phij,jphd->iphd/dot_general | solution.py:69
  104.3 2.7 %all-to-all-done.5 = bf16[32,16,320]{2,1,0:T(8,128)(2,1)} async-done(((bf16[32,16,320]{2,1,0:T(8,128)(2,1)}), bf16[32,16,320]{2,1,0:T(8,128)(2,1)}, u32[]{:S(2)}, u32[]{:S(2)}) %all-to-all-start.5) | async-done | bytes 327712 | tf_op jit(solution)/shard_map/all_to_all | solution.py:123
  107.0 3.6 %all-to-all-start.4 = ((bf16[32,16,320]{2,1,0:T(8,128)(2,1)}), bf16[32,16,320]{2,1,0:T(8,128)(2,1)S(1)}, u32[]{:S(2)}, u32[]{:S(2)}) async-start(bf16[32,16,320]{2,1,0:T(8,128)(2,1)} %reshape.100), calls=%async_computation.4 | async-start | bytes 786432 | tf_op jit(solution)/shard_map/all_to_all | solution.py:122
  110.7 2.5 %fusion.11 = bf16[32,16,4,80]{3,0,2,1:T(8,128)(2,1)} fusion(bf16[32,16,4,80]{3,2,1,0:T(4,128)(2,1)} %reshape.99, f32[16,4,32]{2,1,0:T(4,128)S(1)} %get-tuple-element.17, f32[16,4,32,32]{2,3,1,0:T(8,128)S(1)} %fusion.7), kind=kOutput, calls=%fused_computation.23 | convolution fusion | flops 10848287 | bytes 925696 | tf_op jit(solution)/shard_map/phij,jphd->iphd/dot_general | solution.py:61
  119.3 4.1 %all-to-all-start.7 = ((bf16[32,16,320]{2,1,0:T(8,128)(2,1)}), bf16[32,16,320]{2,1,0:T(8,128)(2,1)}, u32[]{:S(2)}, u32[]{:S(2)}) async-start(bf16[32,16,320]{2,1,0:T(8,128)(2,1)} %reshape.105), calls=%async_computation.7 | async-start | bytes 786432 | tf_op jit(solution)/shard_map/all_to_all | solution.py:121
  126.2 2.2 copy.76
  130.2 2.2 all-to-all-done.7
  135.5 2.3 reshape.104
  142.4 4.6 %copy.78 = f32[640,1280]{1,0:T(8,128)} copy(f32[640,1280]{0,1:T(8,128)} %pad_maximum_fusion) | data formatting | bytes 6553600
  149.9 72.6 %reduce-scatter.9.cloned.1.call-done = f32[80,1280]{1,0:T(8,128)} async-done(((f32[640,1280]{1,0:T(8,128)}), f32[80,1280]{1,0:T(8,128)}) %reduce-scatter.9.cloned.1.call-update) | async-done | bytes 409616
  (87 shorter events, 48.2 us)
Async XLA Ops:
  7.2 9.6 %copy-start = (bf16[640,3,320]{0,2,1:T(8,128)(2,1)S(1)}, bf16[640,3,320]{0,2,1:T(8,128)(2,1)}, u32[]{:S(2)}) copy-start(bf16[640,3,320]{0,2,1:T(8,128)(2,1)} %param.7) | copy-start | bytes 3686404
  7.2 9.4 %copy-start.11 = (bf16[8,64,640]{2,1,0:T(8,128)(2,1)S(1)}, bf16[8,64,640]{2,1,0:T(8,128)(2,1)}, u32[]{:S(2)}) copy-start(bf16[8,64,640]{2,1,0:T(8,128)(2,1)} %param.5) | copy-start | bytes 1966084
  10.0 18.0 %all-to-all-start.2 = ((bf16[8,64,320]{2,0,1:T(8,128)(2,1)}), bf16[8,64,320]{2,0,1:T(8,128)(2,1)S(1)}, u32[]{:S(2)}, u32[]{:S(2)}) async-start(bf16[8,64,320]{2,0,1:T(8,128)(2,1)} %copy.49), calls=%async_computation.2 | async-start | bytes 786432 | tf_op jit(solution)/shard_map/all_to_all | solution.py:115
  28.1 14.3 %all-to-all-start.3 = ((bf16[8,64,320]{2,0,1:T(8,128)(2,1)}), bf16[8,64,320]{2,0,1:T(8,128)(2,1)S(1)}, u32[]{:S(2)}, u32[]{:S(2)}) async-start(bf16[8,64,320]{2,0,1:T(8,128)(2,1)} %copy.51), calls=%async_computation.3 | async-start | bytes 786432 | tf_op jit(solution)/shard_map/all_to_all | solution.py:114
  32.5 26.7 %copy-start.12 = (f32[8,63]{1,0:T(8,128)S(1)}, f32[8,63]{1,0:T(8,128)}, u32[]{:S(2)}) copy-start(f32[8,63]{1,0:T(8,128)} %param.9) | copy-start | bytes 6052
  42.4 13.3 %all-to-all-start.1 = ((bf16[8,64,320]{2,0,1:T(8,128)(2,1)}), bf16[8,64,320]{2,0,1:T(8,128)(2,1)S(1)}, u32[]{:S(2)}, u32[]{:S(2)}) async-start(bf16[8,64,320]{2,0,1:T(8,128)(2,1)} %copy.43), calls=%async_computation.1 | async-start | bytes 786432 | tf_op jit(solution)/shard_map/all_to_all | solution.py:112
  55.7 14.3 %all-to-all-start = ((bf16[8,64,320]{2,0,1:T(8,128)(2,1)}), bf16[8,64,320]{2,0,1:T(8,128)(2,1)S(1)}, u32[]{:S(2)}, u32[]{:S(2)}) async-start(bf16[8,64,320]{2,0,1:T(8,128)(2,1)} %copy.41), calls=%async_computation | async-start | bytes 786432 | tf_op jit(solution)/shard_map/all_to_all | solution.py:113
  70.4 3.4 %copy-start.2 = (bf16[32,16,4,80]{3,2,1,0:T(4,128)(2,1)}, bf16[32,16,4,80]{3,2,1,0:T(4,128)(2,1)S(1)}, u32[]{:S(2)}) copy-start(bf16[32,16,4,80]{3,2,1,0:T(4,128)(2,1)S(1)} %reshape.96) | copy-start | bytes 983044
  78.7 14.4 %all-to-all-start.6 = ((bf16[32,16,320]{2,1,0:T(8,128)(2,1)}), bf16[32,16,320]{2,1,0:T(8,128)(2,1)}, u32[]{:S(2)}, u32[]{:S(2)}) async-start(bf16[32,16,320]{2,1,0:T(8,128)(2,1)} %reshape.102), calls=%async_computation.6 | async-start | bytes 786432 | tf_op jit(solution)/shard_map/all_to_all | solution.py:124
  83.7 3.0 %copy-start.3 = (bf16[32,16,4,80]{3,2,1,0:T(4,128)(2,1)S(1)}, bf16[32,16,4,80]{3,2,1,0:T(4,128)(2,1)}, u32[]{:S(2)}) copy-start(bf16[32,16,4,80]{3,2,1,0:T(4,128)(2,1)} %reshape.97) | copy-start | bytes 983044
  93.0 14.0 %all-to-all-start.5 = ((bf16[32,16,320]{2,1,0:T(8,128)(2,1)}), bf16[32,16,320]{2,1,0:T(8,128)(2,1)}, u32[]{:S(2)}, u32[]{:S(2)}) async-start(bf16[32,16,320]{2,1,0:T(8,128)(2,1)} %reshape.101), calls=%async_computation.5 | async-start | bytes 786432 | tf_op jit(solution)/shard_map/all_to_all | solution.py:123
  107.0 12.3 %all-to-all-start.4 = ((bf16[32,16,320]{2,1,0:T(8,128)(2,1)}), bf16[32,16,320]{2,1,0:T(8,128)(2,1)S(1)}, u32[]{:S(2)}, u32[]{:S(2)}) async-start(bf16[32,16,320]{2,1,0:T(8,128)(2,1)} %reshape.100), calls=%async_computation.4 | async-start | bytes 786432 | tf_op jit(solution)/shard_map/all_to_all | solution.py:122
  116.6 6.9 %copy-start.5 = (bf16[8,4,16,320]{3,2,1,0:T(8,128)(2,1)}, bf16[8,4,16,320]{3,2,1,0:T(8,128)(2,1)S(1)}, u32[]{:S(2)}) copy-start(bf16[8,4,16,320]{3,2,1,0:T(8,128)(2,1)S(1)} %copy.64) | copy-start | bytes 983044
  117.8 5.7 %copy-start.7 = (bf16[8,4,16,320]{3,2,1,0:T(8,128)(2,1)}, bf16[8,4,16,320]{3,2,1,0:T(8,128)(2,1)S(1)}, u32[]{:S(2)}) copy-start(bf16[8,4,16,320]{3,2,1,0:T(8,128)(2,1)S(1)} %copy.61) | copy-start | bytes 983044
  119.3 13.1 %all-to-all-start.7 = ((bf16[32,16,320]{2,1,0:T(8,128)(2,1)}), bf16[32,16,320]{2,1,0:T(8,128)(2,1)}, u32[]{:S(2)}, u32[]{:S(2)}) async-start(bf16[32,16,320]{2,1,0:T(8,128)(2,1)} %reshape.105), calls=%async_computation.7 | async-start | bytes 786432 | tf_op jit(solution)/shard_map/all_to_all | solution.py:121
  123.5 23.6 %reduce-scatter.7.cloned.1.call-start = ((), (), s32[]{:S(2)}) async-start(), calls=%async_computation.10 | async-start | bytes 983040
  123.6 0.8 copy-start.9
  130.1 4.1 %copy-start.6 = (bf16[8,4,16,320]{3,2,1,0:T(8,128)(2,1)S(1)}, bf16[8,4,16,320]{3,2,1,0:T(8,128)(2,1)}, u32[]{:S(2)}) copy-start(bf16[8,4,16,320]{3,2,1,0:T(8,128)(2,1)} %copy-done.5) | copy-start | bytes 983044
  130.1 4.1 %copy-start.8 = (bf16[8,4,16,320]{3,2,1,0:T(8,128)(2,1)S(1)}, bf16[8,4,16,320]{3,2,1,0:T(8,128)(2,1)}, u32[]{:S(2)}) copy-start(bf16[8,4,16,320]{3,2,1,0:T(8,128)(2,1)} %copy-done.7) | copy-start | bytes 983044
  130.1 4.1 %copy-start.10 = (bf16[8,4,16,320]{3,2,1,0:T(8,128)(2,1)S(1)}, bf16[8,4,16,320]{3,2,1,0:T(8,128)(2,1)}, u32[]{:S(2)}) copy-start(bf16[8,4,16,320]{3,2,1,0:T(8,128)(2,1)} %copy-done.9) | copy-start | bytes 983044
  130.1 92.4 %reduce-scatter.9.cloned.1.call-start = ((), (), s32[]{:S(2)}) async-start(), calls=%async_computation.11 | async-start | bytes 3686400
  137.8 1.8 copy-start.1
  147.0 1.9 copy-start.4
Sparse Core Ops, SparseCore 0:
  130.2 9.4 reduce-scatter.6
  147.2 75.3 reduce-scatter.8
where the time goes:
time: 235 us; the launch traced here: 233 us
  waiting for transfers between devices  107 us (46%)
  local copies, waits for them, and re-layouts  47.2 us (20%)
  starting transfers between devices  34.6 us (15%)
  matrix products  25.4 us (11%)
  between operations  14.4 us (6%)
  other arithmetic  4.71 us (2%)
    unnamed x4, waiting for transfers between devices  72.7 us
    unnamed x34, local copies, waits for them, and re-layouts  12.3 us
    all_to_all x1, waiting for transfers between devices, per_device(): lax.all_to_all(value_rows, 'tm', split_axis=1, concat_axis=0, tiled=True)  9.88 us
    all_to_all x1, waiting for transfers between devices, per_device(): lax.all_to_all(grad_attn, 'tm', split_axis=1, concat_axis=0, tiled=True)  9.01 us
    all_to_all x1, waiting for transfers between devices, per_device(): lax.all_to_all(query_rows, 'tm', split_axis=1, concat_axis=0, tiled=True)  8.82 us
    all_to_all x1, starting transfers between devices, per_device(): lax.all_to_all(grad_attn, 'tm', split_axis=1, concat_axis=0, tiled=True)  6.32 us
    gather x2, local copies, waits for them, and re-layouts, bias_table(): return bias_rows[:, offsets]  5.38 us
    all_to_all x1, starting transfers between devices, per_device(): lax.all_to_all(grad_value, 'tm', split_axis=0, concat_axis=1, tiled=True)  5.05 us
  transfers between devices with their start and end apart: 10, of which 8 were waited for; matrix products, arithmetic and copies ran while one was open for 26% of the time, Pallas kernels for 0%

commit v1 on v0

--- a/solution.py
+++ b/solution.py
@@ -5,6 +5,28 @@
 from jax.sharding import PartitionSpec as P
 
 H = 8
+
+
+def in_blocks(x, dim, size):
+    before, after = (x.shape[:dim], x.shape[dim + 1 :])
+    return jnp.moveaxis(x.reshape(*before, size, -1, *after), dim, 0)
+
+
+def joined_along(blocks, dim):
+    dims = list(blocks.shape[1:])
+    dims[dim] *= blocks.shape[0]
+    return jnp.moveaxis(blocks, 0, dim).reshape(dims)
+
+
+def exchange_directly(shard, axis, split_dim, concat_dim):
+    devices, here = (lax.axis_size(axis), lax.axis_index(axis))
+    blocks = in_blocks(shard, split_dim, devices)
+    outs = [blocks[here]]
+    for hop in range(1, devices):
+        sent = blocks[(here + hop) % devices]
+        outs.append(lax.ppermute(sent, axis, [(i, (i + hop) % devices) for i in range(devices)]))
+    blocks = jnp.stack(outs)[(here - jnp.arange(devices)) % devices]
+    return joined_along(blocks, concat_dim)
 
 
 def positional(frame_pos, channels):
@@ -120,7 +142,7 @@
     attn_out, grad_query, grad_key, grad_value = (
         lax.all_to_all(attn_out, "tm", split_axis=0, concat_axis=1, tiled=True),
         lax.all_to_all(grad_query, "tm", split_axis=0, concat_axis=1, tiled=True),
-        lax.all_to_all(grad_key, "tm", split_axis=0, concat_axis=1, tiled=True),
+        exchange_directly(grad_key, "tm", 0, 1),
         lax.all_to_all(grad_value, "tm", split_axis=0, concat_axis=1, tiled=True),
     )
     grad_qkv = jnp.stack((grad_query, grad_key, grad_value), axis=2)

time: 235 us -> 237 us (level)
    all_to_all x1 -> x0, starting transfers between devices: 4.98 us -> none  [per_device(): lax.all_to_all(grad_key, 'tm', split_axis=0, concat_axis=1, tiled=True)]
    ppermute x0 -> x3, starting transfers between devices: none -> 4.95 us  [exchange_directly(): lax.ppermute(sent, axis, [(i, (i + hop) % devices) for i in range(devices)])]
    all_to_all x1 -> x0, waiting for transfers between devices: 2.71 us -> none  [per_device(): lax.all_to_all(grad_key, 'tm', split_axis=0, concat_axis=1, tiled=True)]
    ppermute x0 -> x3, waiting for transfers between devices: none -> 2.69 us  [exchange_directly(): lax.ppermute(sent, axis, [(i, (i + hop) % devices) for i in range(devices)])]
    unnamed x34 -> x36, local copies, waits for them, and re-layouts: 12.3 us -> 12.3 us
  transfers between devices with their start and end apart: 10 -> 12, of which waited for: 8 -> 7; matrix products, arithmetic and copies ran while one was open for 26% -> 26% of each run, Pallas kernels for 0% -> 0%
where the time goes in v1:
time: 237 us; the launch traced here: 235 us
  waiting for transfers between devices  105 us (44%)
  local copies, waits for them, and re-layouts  47.8 us (20%)
  starting transfers between devices  36.6 us (15%)
  matrix products  24.5 us (10%)
  between operations  14.5 us (6%)
  other arithmetic  6.43 us (3%)
    unnamed x4, waiting for transfers between devices  73.6 us
    unnamed x36, local copies, waits for them, and re-layouts  12.3 us
    all_to_all x1, waiting for transfers between devices, per_device(): lax.all_to_all(value_rows, 'tm', split_axis=1, concat_axis=0, tiled=True)  9.87 us
    all_to_all x1, waiting for transfers between devices, per_device(): lax.all_to_all(grad_attn, 'tm', split_axis=1, concat_axis=0, tiled=True)  9 us
    all_to_all x1, waiting for transfers between devices, per_device(): lax.all_to_all(query_rows, 'tm', split_axis=1, concat_axis=0, tiled=True)  8.83 us
    all_to_all x1, starting transfers between devices, per_device(): lax.all_to_all(grad_attn, 'tm', split_axis=1, concat_axis=0, tiled=True)  6.32 us
    gather x2, local copies, waits for them, and re-layouts, bias_table(): return bias_rows[:, offsets]  5.37 us
    all_to_all x1, starting transfers between devices, per_device(): lax.all_to_all(grad_query, 'tm', split_axis=0, concat_axis=1, tiled=True)  5.09 us
  transfers between devices with their start and end apart: 12, of which 7 were waited for; matrix products, arithmetic and copies ran while one was open for 26% of the time, Pallas kernels for 0%

profile of v1, /device:TPU:0, one launch (start us, length us, event | category | flops | bytes accessed | tf_op | source)
XLA Modules:
  0.0 235.2 jit_solution(5839023219279873113)
XLA Ops:
  10.0 6.3 %all-to-all-start.2 = ((bf16[8,64,320]{2,0,1:T(8,128)(2,1)}), bf16[8,64,320]{2,0,1:T(8,128)(2,1)S(1)}, u32[]{:S(2)}, u32[]{:S(2)}) async-start(bf16[8,64,320]{2,0,1:T(8,128)(2,1)} %copy.49), calls=%async_computation.2 | async-start | bytes 786432 | tf_op jit(solution)/shard_map/all_to_all | solution.py:137
  19.0 9.0 %all-to-all-done.2 = bf16[8,64,320]{2,0,1:T(8,128)(2,1)S(1)} async-done(((bf16[8,64,320]{2,0,1:T(8,128)(2,1)}), bf16[8,64,320]{2,0,1:T(8,128)(2,1)S(1)}, u32[]{:S(2)}, u32[]{:S(2)}) %all-to-all-start.2) | async-done | bytes 327712 | tf_op jit(solution)/shard_map/all_to_all | solution.py:137
  28.1 3.5 %all-to-all-start.3 = ((bf16[8,64,320]{2,0,1:T(8,128)(2,1)}), bf16[8,64,320]{2,0,1:T(8,128)(2,1)S(1)}, u32[]{:S(2)}, u32[]{:S(2)}) async-start(bf16[8,64,320]{2,0,1:T(8,128)(2,1)} %copy.51), calls=%async_computation.3 | async-start | bytes 786432 | tf_op jit(solution)/shard_map/all_to_all | solution.py:136
  32.5 9.9 %all-to-all-done.3 = bf16[8,64,320]{2,0,1:T(8,128)(2,1)S(1)} async-done(((bf16[8,64,320]{2,0,1:T(8,128)(2,1)}), bf16[8,64,320]{2,0,1:T(8,128)(2,1)S(1)}, u32[]{:S(2)}, u32[]{:S(2)}) %all-to-all-start.3) | async-done | bytes 327712 | tf_op jit(solution)/shard_map/all_to_all | solution.py:136
  42.4 3.5 %all-to-all-start.1 = ((bf16[8,64,320]{2,0,1:T(8,128)(2,1)}), bf16[8,64,320]{2,0,1:T(8,128)(2,1)S(1)}, u32[]{:S(2)}, u32[]{:S(2)}) async-start(bf16[8,64,320]{2,0,1:T(8,128)(2,1)} %copy.43), calls=%async_computation.1 | async-start | bytes 786432 | tf_op jit(solution)/shard_map/all_to_all | solution.py:134
  46.8 8.8 %all-to-all-done.1 = bf16[8,64,320]{2,0,1:T(8,128)(2,1)S(1)} async-done(((bf16[8,64,320]{2,0,1:T(8,128)(2,1)}), bf16[8,64,320]{2,0,1:T(8,128)(2,1)S(1)}, u32[]{:S(2)}, u32[]{:S(2)}) %all-to-all-start.1) | async-done | bytes 327712 | tf_op jit(solution)/shard_map/all_to_all | solution.py:134
  55.7 4.1 %all-to-all-start = ((bf16[8,64,320]{2,0,1:T(8,128)(2,1)}), bf16[8,64,320]{2,0,1:T(8,128)(2,1)}, u32[]{:S(2)}, u32[]{:S(2)}) async-start(bf16[8,64,320]{2,0,1:T(8,128)(2,1)} %copy.41), calls=%async_computation | async-start | bytes 786432 | tf_op jit(solution)/shard_map/all_to_all | solution.py:135
  60.0 4.0 %gather_fusion = f32[1024,4]{1,0:T(8,128)} fusion(f32[4,63]{0,1:T(8,128)S(1)} %copy.80, s32[1024]{0:T(1024)S(1)} %broadcast_clamp_fusion), kind=kCustom, calls=%fused_computation | custom fusion | bytes 36864 | tf_op jit(solution)/shard_map/gather | solution.py:46
  71.2 1.9 fusion.7
  74.3 2.5 %fusion.13 = bf16[32,16,4,80]{3,0,2,1:T(8,128)(2,1)} fusion(bf16[32,16,4,80]{3,2,1,0:T(4,128)(2,1)} %reshape.143, f32[16,4,32]{2,1,0:T(4,128)S(1)} %get-tuple-element.21, f32[16,4,32,32]{2,3,1,0:T(8,128)S(1)} %fusion.7), kind=kOutput, calls=%fused_computation.26 | convolution fusion | flops 10848287 | bytes 925696 | tf_op jit(solution)/shard_map/phij,iphd->jphd/dot_general | solution.py:97
  79.2 5.0 %all-to-all-start.5 = ((bf16[32,16,320]{2,1,0:T(8,128)(2,1)}), bf16[32,16,320]{2,1,0:T(8,128)(2,1)}, u32[]{:S(2)}, u32[]{:S(2)}) async-start(bf16[32,16,320]{2,1,0:T(8,128)(2,1)} %reshape.146), calls=%async_computation.5 | async-start | bytes 786432 | tf_op jit(solution)/shard_map/all_to_all | solution.py:146
  84.3 3.0 %fusion.27 = f32[16,4,32,32]{2,3,1,0:T(8,128)} fusion(bf16[32,16,4,80]{3,2,1,0:T(4,128)(2,1)} %reshape.144, bf16[32,16,4,80]{3,2,1,0:T(4,128)(2,1)} %reshape.143), kind=kOutput, calls=%fused_computation.40 | convolution fusion | flops 10485760 | bytes 917504 | tf_op jit(solution)/shard_map/iphd,jphd->phij/dot_general | solution.py:86
  87.3 3.7 %fusion.10 = bf16[32,16,4,80]{3,0,2,1:T(8,128)(2,1)} fusion(f32[16,4,32,32]{2,3,1,0:T(8,128)} %fusion.27, bf16[32,16,4,80]{3,2,1,0:T(4,128)(2,1)S(1)} %copy-done.3, f32[16,4,32,32]{2,3,1,0:T(8,128)} %get-tuple-element.22, f32[16,4,32]{2,1,0:T(4,128)S(1)} %get-tuple-element.21), kind=kOutput, calls=%fused_computation.23 | convolution fusion | flops 11110431 | bytes 1187840 | tf_op jit(solution)/shard_map/phij,jphd->iphd/dot_general | solution.py:91
  93.4 5.1 %all-to-all-start.4 = ((bf16[32,16,320]{2,1,0:T(8,128)(2,1)}), bf16[32,16,320]{2,1,0:T(8,128)(2,1)}, u32[]{:S(2)}, u32[]{:S(2)}) async-start(bf16[32,16,320]{2,1,0:T(8,128)(2,1)} %reshape.145), calls=%async_computation.4 | async-start | bytes 786432 | tf_op jit(solution)/shard_map/all_to_all | solution.py:144
  98.5 3.9 %fusion.12 = bf16[32,16,4,80]{3,0,2,1:T(8,128)(2,1)} fusion(f32[16,4,32,32]{2,3,1,0:T(8,128)} %fusion.27, bf16[32,16,4,80]{3,2,1,0:T(4,128)(2,1)} %copy-done.2, f32[16,4,32,32]{2,3,1,0:T(8,128)} %get-tuple-element.22, f32[16,4,32]{2,1,0:T(4,128)S(1)} %get-tuple-element.21), kind=kOutput, calls=%fused_computation.25 | convolution fusion | flops 11110431 | bytes 1187840 | tf_op jit(solution)/shard_map/phij,iphd->jphd/dot_general | solution.py:94
  106.6 3.8 %collective-permute-start.2 = (bf16[8,16,320]{2,1,0:T(8,128)(2,1)}, bf16[8,16,320]{2,1,0:T(8,128)(2,1)}, u32[]{:S(2)}, u32[]{:S(2)}) collective-permute-start(bf16[8,16,320]{2,1,0:T(8,128)(2,1)} %get-tuple-element.16), channel_id=1, source_target_pairs={{0,12},{4,0},{8,4},{12,8},{1,13},{5,1},{9,5},{13,9},{2,14},{6,2},{... | collective-permute-start | bytes 245768 | tf_op jit(solution)/shard_map/ppermute | solution.py:27
  114.6 2.7 %collective-permute-done.1 = bf16[8,16,320]{2,1,0:T(8,128)(2,1)} collective-permute-done((bf16[8,16,320]{2,1,0:T(8,128)(2,1)}, bf16[8,16,320]{2,1,0:T(8,128)(2,1)}, u32[]{:S(2)}, u32[]{:S(2)}) %collective-permute-start.1) | collective-permute-done | bytes 81952 | tf_op jit(solution)/shard_map/ppermute | solution.py:27
  120.4 4.1 %all-to-all-start.6 = ((bf16[32,16,320]{2,1,0:T(8,128)(2,1)}), bf16[32,16,320]{2,1,0:T(8,128)(2,1)}, u32[]{:S(2)}, u32[]{:S(2)}) async-start(bf16[32,16,320]{2,1,0:T(8,128)(2,1)} %reshape.149), calls=%async_computation.6 | async-start | bytes 786432 | tf_op jit(solution)/shard_map/all_to_all | solution.py:143
  126.4 1.9 fusion.8
  128.3 2.2 copy.76
  136.5 2.3 reshape.148
  141.7 1.9 pad_maximum_fusion
  143.6 4.6 %copy.78 = f32[640,1280]{1,0:T(8,128)} copy(f32[640,1280]{0,1:T(8,128)} %pad_maximum_fusion) | data formatting | bytes 6553600
  151.1 73.5 %reduce-scatter.9.cloned.1.call-done = f32[80,1280]{1,0:T(8,128)} async-done(((f32[640,1280]{1,0:T(8,128)}), f32[80,1280]{1,0:T(8,128)}) %reduce-scatter.9.cloned.1.call-update) | async-done | bytes 409616
  (98 shorter events, 49.5 us)
Async XLA Ops:
  7.2 9.6 %copy-start = (bf16[640,3,320]{0,2,1:T(8,128)(2,1)S(1)}, bf16[640,3,320]{0,2,1:T(8,128)(2,1)}, u32[]{:S(2)}) copy-start(bf16[640,3,320]{0,2,1:T(8,128)(2,1)} %param.7) | copy-start | bytes 3686404
  7.2 9.4 %copy-start.11 = (bf16[8,64,640]{2,1,0:T(8,128)(2,1)S(1)}, bf16[8,64,640]{2,1,0:T(8,128)(2,1)}, u32[]{:S(2)}) copy-start(bf16[8,64,640]{2,1,0:T(8,128)(2,1)} %param.5) | copy-start | bytes 1966084
  10.0 18.0 %all-to-all-start.2 = ((bf16[8,64,320]{2,0,1:T(8,128)(2,1)}), bf16[8,64,320]{2,0,1:T(8,128)(2,1)S(1)}, u32[]{:S(2)}, u32[]{:S(2)}) async-start(bf16[8,64,320]{2,0,1:T(8,128)(2,1)} %copy.49), calls=%async_computation.2 | async-start | bytes 786432 | tf_op jit(solution)/shard_map/all_to_all | solution.py:137
  28.1 14.3 %all-to-all-start.3 = ((bf16[8,64,320]{2,0,1:T(8,128)(2,1)}), bf16[8,64,320]{2,0,1:T(8,128)(2,1)S(1)}, u32[]{:S(2)}, u32[]{:S(2)}) async-start(bf16[8,64,320]{2,0,1:T(8,128)(2,1)} %copy.51), calls=%async_computation.3 | async-start | bytes 786432 | tf_op jit(solution)/shard_map/all_to_all | solution.py:136
  32.5 27.3 %copy-start.13 = (f32[8,63]{1,0:T(8,128)S(1)}, f32[8,63]{1,0:T(8,128)}, u32[]{:S(2)}) copy-start(f32[8,63]{1,0:T(8,128)} %param.9) | copy-start | bytes 6052
  42.4 13.3 %all-to-all-start.1 = ((bf16[8,64,320]{2,0,1:T(8,128)(2,1)}), bf16[8,64,320]{2,0,1:T(8,128)(2,1)S(1)}, u32[]{:S(2)}, u32[]{:S(2)}) async-start(bf16[8,64,320]{2,0,1:T(8,128)(2,1)} %copy.43), calls=%async_computation.1 | async-start | bytes 786432 | tf_op jit(solution)/shard_map/all_to_all | solution.py:134
  55.7 13.3 %all-to-all-start = ((bf16[8,64,320]{2,0,1:T(8,128)(2,1)}), bf16[8,64,320]{2,0,1:T(8,128)(2,1)}, u32[]{:S(2)}, u32[]{:S(2)}) async-start(bf16[8,64,320]{2,0,1:T(8,128)(2,1)} %copy.41), calls=%async_computation | async-start | bytes 786432 | tf_op jit(solution)/shard_map/all_to_all | solution.py:135
  68.8 4.3 %copy-start.2 = (bf16[32,16,4,80]{3,2,1,0:T(4,128)(2,1)}, bf16[32,16,4,80]{3,2,1,0:T(4,128)(2,1)S(1)}, u32[]{:S(2)}) copy-start(bf16[32,16,4,80]{3,2,1,0:T(4,128)(2,1)S(1)} %reshape.142) | copy-start | bytes 983044
  74.3 24.2 %copy-start.12 = (f32[16,4,32]{2,1,0:T(4,128)}, f32[16,4,32]{2,1,0:T(4,128)S(1)}, u32[]{:S(2)}) copy-start(f32[16,4,32]{2,1,0:T(4,128)S(1)} %get-tuple-element.21) | copy-start | bytes 24580
  79.2 14.2 %all-to-all-start.5 = ((bf16[32,16,320]{2,1,0:T(8,128)(2,1)}), bf16[32,16,320]{2,1,0:T(8,128)(2,1)}, u32[]{:S(2)}, u32[]{:S(2)}) async-start(bf16[32,16,320]{2,1,0:T(8,128)(2,1)} %reshape.146), calls=%async_computation.5 | async-start | bytes 786432 | tf_op jit(solution)/shard_map/all_to_all | solution.py:146
  84.3 3.0 %copy-start.3 = (bf16[32,16,4,80]{3,2,1,0:T(4,128)(2,1)S(1)}, bf16[32,16,4,80]{3,2,1,0:T(4,128)(2,1)}, u32[]{:S(2)}) copy-start(bf16[32,16,4,80]{3,2,1,0:T(4,128)(2,1)} %reshape.141) | copy-start | bytes 983044
  93.4 27.0 %all-to-all-start.4 = ((bf16[32,16,320]{2,1,0:T(8,128)(2,1)}), bf16[32,16,320]{2,1,0:T(8,128)(2,1)}, u32[]{:S(2)}, u32[]{:S(2)}) async-start(bf16[32,16,320]{2,1,0:T(8,128)(2,1)} %reshape.145), calls=%async_computation.4 | async-start | bytes 786432 | tf_op jit(solution)/shard_map/all_to_all | solution.py:144
  106.6 8.0 %collective-permute-start.2 = (bf16[8,16,320]{2,1,0:T(8,128)(2,1)}, bf16[8,16,320]{2,1,0:T(8,128)(2,1)}, u32[]{:S(2)}, u32[]{:S(2)}) collective-permute-start(bf16[8,16,320]{2,1,0:T(8,128)(2,1)} %get-tuple-element.16), channel_id=1, source_target_pairs={{0,12},{4,0},{8,4},{12,8},{1,13},{5,1},{9,5},{13,9},{2,14},{6,2},{... | collective-permute-start | bytes 245768 | tf_op jit(solution)/shard_map/ppermute | solution.py:27
  110.4 6.9 %collective-permute-start.1 = (bf16[8,16,320]{2,1,0:T(8,128)(2,1)}, bf16[8,16,320]{2,1,0:T(8,128)(2,1)}, u32[]{:S(2)}, u32[]{:S(2)}) collective-permute-start(bf16[8,16,320]{2,1,0:T(8,128)(2,1)} %get-tuple-element.17), channel_id=1, source_target_pairs={{0,8},{4,12},{8,0},{12,4},{1,9},{5,13},{9,1},{13,5},{2,10},{6,14},... | collective-permute-start | bytes 245768 | tf_op jit(solution)/shard_map/ppermute | solution.py:27
  110.4 6.9 %collective-permute-start = (bf16[8,16,320]{2,1,0:T(8,128)(2,1)}, bf16[8,16,320]{2,1,0:T(8,128)(2,1)}, u32[]{:S(2)}, u32[]{:S(2)}) collective-permute-start(bf16[8,16,320]{2,1,0:T(8,128)(2,1)} %get-tuple-element.18), channel_id=1, source_target_pairs={{0,4},{4,8},{8,12},{12,0},{1,5},{5,9},{9,13},{13,1},{2,6},{6,10},{... | collective-permute-start | bytes 245768 | tf_op jit(solution)/shard_map/ppermute | solution.py:27
  119.2 6.5 %copy-start.5 = (bf16[8,4,16,320]{3,2,1,0:T(8,128)(2,1)}, bf16[8,4,16,320]{3,2,1,0:T(8,128)(2,1)S(1)}, u32[]{:S(2)}) copy-start(bf16[8,4,16,320]{3,2,1,0:T(8,128)(2,1)S(1)} %copy.61) | copy-start | bytes 983044
  120.4 5.3 %copy-start.7 = (bf16[8,4,16,320]{3,2,1,0:T(8,128)(2,1)}, bf16[8,4,16,320]{3,2,1,0:T(8,128)(2,1)S(1)}, u32[]{:S(2)}) copy-start(bf16[8,4,16,320]{3,2,1,0:T(8,128)(2,1)S(1)} %copy.64) | copy-start | bytes 983044
  120.4 13.1 %all-to-all-start.6 = ((bf16[32,16,320]{2,1,0:T(8,128)(2,1)}), bf16[32,16,320]{2,1,0:T(8,128)(2,1)}, u32[]{:S(2)}, u32[]{:S(2)}) async-start(bf16[32,16,320]{2,1,0:T(8,128)(2,1)} %reshape.149), calls=%async_computation.6 | async-start | bytes 786432 | tf_op jit(solution)/shard_map/all_to_all | solution.py:143
  124.5 23.7 %reduce-scatter.7.cloned.1.call-start = ((), (), s32[]{:S(2)}) async-start(), calls=%async_computation.9 | async-start | bytes 983040
  132.1 3.1 %copy-start.6 = (bf16[8,4,16,320]{3,2,1,0:T(8,128)(2,1)S(1)}, bf16[8,4,16,320]{3,2,1,0:T(8,128)(2,1)}, u32[]{:S(2)}) copy-start(bf16[8,4,16,320]{3,2,1,0:T(8,128)(2,1)} %copy-done.5) | copy-start | bytes 983044
  132.1 3.1 %copy-start.8 = (bf16[8,4,16,320]{3,2,1,0:T(8,128)(2,1)S(1)}, bf16[8,4,16,320]{3,2,1,0:T(8,128)(2,1)}, u32[]{:S(2)}) copy-start(bf16[8,4,16,320]{3,2,1,0:T(8,128)(2,1)} %copy-done.7) | copy-start | bytes 983044
  132.1 3.1 %copy-start.10 = (bf16[8,4,16,320]{3,2,1,0:T(8,128)(2,1)S(1)}, bf16[8,4,16,320]{3,2,1,0:T(8,128)(2,1)}, u32[]{:S(2)}) copy-start(bf16[8,4,16,320]{3,2,1,0:T(8,128)(2,1)} %copy-done.9) | copy-start | bytes 983044
  132.2 92.4 %reduce-scatter.9.cloned.1.call-start = ((), (), s32[]{:S(2)}) async-start(), calls=%async_computation.10 | async-start | bytes 3686400
  148.2 1.9 copy-start.4
  (2 other events, 2.6 us)
Sparse Core Ops, SparseCore 0:
  132.3 9.4 reduce-scatter.6
  148.3 76.2 reduce-scatter.8
